TPU v7x, 32 devices: a whole 2x2x4 slice. The times are simulated.
32 devices in a mesh: seq: 8 (over z, y), ch: 4 (over x, core).
Axes of the slice: x: 2, y: 2, z: 4, core: 2. Of those that a mesh axis runs over, the one named last changes fastest.
Arguments:
- queries: float32 [1024, 1024], P('seq', 'ch'), may hold values from -6 to 6
- keys: float32 [1024, 1024], P('seq', 'ch'), may hold values from -6 to 6
- values: float32 [1024, 1024], P('seq', 'ch'), may hold values from -6 to 6
- filters: float32 [1024, 1024], P('seq', 'ch'), may hold values from -0.375 to 0.375
- short_w: float32 [3, 1024], P(None, 'ch'), may hold values from -3.5 to 3.5
- bias: float32 [1024], P('ch'), may hold values from -4 to 4
Outputs:
- mixed: float32 [1024, 1024], P('seq', 'ch')
All inputs are finite; a program needn't handle non-finite values.
Results may differ from a plain program's by a relative error of at most 0.00011.
Values sent between devices are 32-bit elements; how exact they have to be, the bound alone decides.
A program may use at most 64 MiB of HBM per device.

v0:
```python
import math

import jax
import jax.numpy as jnp
from jax import lax
from jax.sharding import PartitionSpec as P


def passed_along(block, axis, distance):
    devices = range(lax.axis_size(axis))
    route = [(i - distance, i) for i in devices if i - distance in devices]
    return lax.ppermute(block, axis, route)


def angles(index, modulus, sign):
    turned = (index % modulus).astype(jnp.float32) * (2.0 * math.pi / modulus)
    return (jnp.cos(turned), sign * jnp.sin(turned))


def complex_mix(form, mat_real, mat_imag, data_real, data_imag):
    first = jnp.einsum(form, mat_real, data_real, precision=lax.Precision.HIGHEST)
    second = jnp.einsum(form, mat_imag, data_imag, precision=lax.Precision.HIGHEST)
    third = jnp.einsum(form, mat_real, data_imag, precision=lax.Precision.HIGHEST)
    fourth = jnp.einsum(form, mat_imag, data_real, precision=lax.Precision.HIGHEST)
    return (first - second, third + fourth)


def body(queries, keys, values, filters, short_w, bias):
    row_count, channels = queries.shape
    shards = lax.axis_size("seq")
    device = lax.axis_index("seq")
    slab = row_count // shards
    total = row_count * shards
    stacked = jnp.stack((queries, keys, values))
    earlier = passed_along(stacked[:, row_count - 2 :, :], "seq", 1)
    extended = jnp.concatenate((earlier, stacked), axis=1)
    shorted = (
        short_w[0] * extended[:, 2:]
        + short_w[1] * extended[:, 1:-1]
        + short_w[2] * extended[:, :-2]
    )
    gated = shorted[1] * shorted[2]
    signal = jnp.stack((gated, filters))
    within = device * slab + jnp.arange(slab, dtype=jnp.int32)
    column_index = jnp.arange(shards, dtype=jnp.int32)
    row_index = jnp.arange(row_count, dtype=jnp.int32)
    own_pos = row_count * device + row_index
    cosine, sine = angles(own_pos, 2 * total, -1.0)
    lifted = jnp.stack((signal, signal * cosine[:, None], signal * sine[:, None]), axis=1)[
        :, :, None
    ]
    received = lax.all_to_all(lifted, "seq", split_axis=3, concat_axis=2, tiled=True)
    real_part = jnp.stack((received[:, 0], received[:, 1]), axis=1)
    imag_part = jnp.stack((jnp.zeros_like(received[:, 0]), received[:, 2]), axis=1)
    freq_cos, freq_sin = angles(column_index[:, None] * column_index[None, :], shards, -1.0)
    real_part, imag_part = complex_mix("kd,srdmc->srkmc", freq_cos, freq_sin, real_part, imag_part)
    twist_cos, twist_sin = angles(column_index[:, None] * within[None, :], total, -1.0)
    twist_cos = twist_cos[:, :, None]
    twist_sin = twist_sin[:, :, None]
    real_part, imag_part = (
        real_part * twist_cos - imag_part * twist_sin,
        real_part * twist_sin + imag_part * twist_cos,
    )
    square_index = row_index[:, None] * row_index[None, :]
    long_cos, long_sin = angles(square_index, row_count, -1.0)
    pair = (
        lax.all_to_all(real_part, "seq", split_axis=2, concat_axis=3, tiled=True),
        lax.all_to_all(imag_part, "seq", split_axis=2, concat_axis=3, tiled=True),
    )
    spec_real, spec_imag = complex_mix("km,srjmc->srjkc", long_cos, long_sin, pair[0], pair[1])
    prod_real = spec_real[0] * spec_real[1] - spec_imag[0] * spec_imag[1]
    prod_imag = spec_real[0] * spec_imag[1] + spec_imag[0] * spec_real[1]
    inverse_cos, inverse_sin = angles(square_index, row_count, 1.0)
    back_real, back_imag = complex_mix(
        "mk,rjkc->rjmc", inverse_cos, inverse_sin, prod_real, prod_imag
    )
    undo_cos, undo_sin = angles(device * row_index, total, 1.0)
    undo_cos = undo_cos[:, None]
    undo_sin = undo_sin[:, None]
    back_real, back_imag = (
        back_real * undo_cos - back_imag * undo_sin,
        back_real * undo_sin + back_imag * undo_cos,
    )
    column_cos, column_sin = angles(column_index[:, None] * column_index[None, :], shards, 1.0)
    pair = (
        lax.all_to_all(back_real, "seq", split_axis=2, concat_axis=1, tiled=True),
        lax.all_to_all(back_imag, "seq", split_axis=2, concat_axis=1, tiled=True),
    )
    inv_real, inv_imag = complex_mix("dk,rkmc->rdmc", column_cos, column_sin, pair[0], pair[1])
    factor = 0.5 / total
    packed = jnp.stack((inv_real[0], inv_imag[0], inv_real[1], inv_imag[1]))
    landed = lax.all_to_all(packed, "seq", split_axis=1, concat_axis=2, tiled=True)
    cosine, sine = angles(own_pos, 2 * total, 1.0)
    long_part = factor * (
        landed[0, 0] + cosine[:, None] * landed[2, 0] - sine[:, None] * landed[3, 0]
    )
    return shorted[0] * (long_part + bias * gated)


def solution(mesh):
    placed = (
        P("seq", "ch"),
        P("seq", "ch"),
        P("seq", "ch"),
        P("seq", "ch"),
        P(None, "ch"),
        P("ch"),
    )
    return jax.shard_map(
        body, mesh=mesh, in_specs=placed, out_specs=P("seq", "ch"), check_vma=False
    )
```

profile of v0, /device:TPU:0, one launch (start us, length us, event | category | flops | bytes accessed | tf_op | source)
XLA Modules:
  0.0 130.0 jit_solution(9830155882568192317)
XLA Ops:
  0.0 0.0 copy-start
  0.0 0.0 copy-start.1
  0.0 0.0 copy-start.2
  0.0 1.1 pad_maximum_fusion.1
  1.1 0.0 copy-start.4
  1.1 4.9 %collective-permute-start = (f32[3,2,256]{2,1,0:T(2,128)S(1)}, f32[3,2,256]{2,1,0:T(2,128)S(1)}, u32[]{:S(2)}, u32[]{:S(2)}) collective-permute-start(f32[3,2,256]{2,1,0:T(2,128)S(1)} %slice.95), channel_id=1, source_target_pairs={{0,4},{4,8},{8,12},{12,16},{16,20},{20,24},{24,28},{1,5},{5,9},{9,... | collective-permute-start | bytes 18440 | tf_op jit(solution)/shard_map/ppermute | solution.py:12
  6.1 0.0 copy-done.4
  6.1 0.1 fusion.109
  6.1 0.1 broadcast_multiply_fusion
  6.2 1.2 collective-permute-done
  7.4 0.0 copy-done
  7.4 0.0 copy-done.1
  7.4 0.0 copy-done.2
  7.4 0.1 fusion.12
  7.6 0.0 copy-start.3
  7.6 0.9 copy-done.3
  8.5 0.1 fusion.29
  8.6 0.1 maximum_bitcast_fusion
  8.7 1.5 %copy.53 = f32[2,3,1,128,256]{4,0,2,1,3:T(2,128)} copy(f32[2,3,1,128,256]{4,3,1,0,2:T(8,128)S(1)} %maximum_bitcast_fusion) | data formatting | bytes 1572864 | tf_op jit(solution)/shard_map/broadcast_in_dim | solution.py:49
  10.2 6.6 %all-to-all-start = ((f32[2,3,1,128,256]{4,0,2,1,3:T(2,128)}), f32[2,3,1,128,256]{4,0,2,1,3:T(2,128)S(1)}, u32[]{:S(2)}, u32[]{:S(2)}) async-start(f32[2,3,1,128,256]{4,0,2,1,3:T(2,128)} %copy.53), calls=%async_computation | async-start | bytes 1572864 | tf_op jit(solution)/shard_map/all_to_all | solution.py:52
  16.8 0.1 fusion.82
  16.9 19.0 %all-to-all-done = f32[2,3,1,128,256]{4,0,2,1,3:T(2,128)S(1)} async-done(((f32[2,3,1,128,256]{4,0,2,1,3:T(2,128)}), f32[2,3,1,128,256]{4,0,2,1,3:T(2,128)S(1)}, u32[]{:S(2)}, u32[]{:S(2)}) %all-to-all-start) | async-done | bytes 786464 | tf_op jit(solution)/shard_map/all_to_all | solution.py:52
  35.9 0.1 copy.54
  36.0 0.9 fusion.10
  36.9 0.9 fusion.8
  37.8 0.7 fusion.1
  38.5 0.8 multiply_subtract_fusion
  39.3 1.0 copy.57
  40.3 3.5 %all-to-all-start.1 = ((f32[2,2,8,16,256]{4,3,1,0,2:T(8,128)}), f32[2,2,8,16,256]{4,3,1,0,2:T(8,128)S(1)}, u32[]{:S(2)}, u32[]{:S(2)}) async-start(f32[2,2,8,16,256]{4,3,1,0,2:T(8,128)} %copy.57), calls=%async_computation.1 | async-start | bytes 1048576 | tf_op jit(solution)/shard_map/all_to_all | solution.py:67
  43.8 1.0 copy.60
  44.8 13.4 %all-to-all-done.1 = f32[2,2,8,16,256]{4,3,1,0,2:T(8,128)S(1)} async-done(((f32[2,2,8,16,256]{4,3,1,0,2:T(8,128)}), f32[2,2,8,16,256]{4,3,1,0,2:T(8,128)S(1)}, u32[]{:S(2)}, u32[]{:S(2)}) %all-to-all-start.1) | async-done | bytes 524320 | tf_op jit(solution)/shard_map/all_to_all | solution.py:67
  58.2 3.7 %all-to-all-start.2 = ((f32[2,2,8,16,256]{4,3,1,0,2:T(8,128)}), f32[2,2,8,16,256]{4,3,1,0,2:T(8,128)S(1)}, u32[]{:S(2)}, u32[]{:S(2)}) async-start(f32[2,2,8,16,256]{4,3,1,0,2:T(8,128)} %copy.60), calls=%async_computation.2 | async-start | bytes 1048576 | tf_op jit(solution)/shard_map/all_to_all | solution.py:68
  61.9 0.1 fusion.106
  62.0 1.1 fusion.46
  63.1 13.4 %all-to-all-done.2 = f32[2,2,8,16,256]{4,3,1,0,2:T(8,128)S(1)} async-done(((f32[2,2,8,16,256]{4,3,1,0,2:T(8,128)}), f32[2,2,8,16,256]{4,3,1,0,2:T(8,128)S(1)}, u32[]{:S(2)}, u32[]{:S(2)}) %all-to-all-start.2) | async-done | bytes 524320 | tf_op jit(solution)/shard_map/all_to_all | solution.py:68
  76.5 1.1 fusion.44
  77.6 1.1 fusion.3
  78.8 1.1 fusion.2
  79.9 0.1 multiply_subtract_fusion.1
  80.0 0.6 fusion.14
  80.6 0.6 fusion.18
  81.2 0.6 fusion.6
  81.8 0.6 subtract_bitcast_fusion
  82.5 0.8 copy.65
  83.3 3.6 %all-to-all-start.3 = ((f32[2,1,128,256]{3,0,1,2:T(2,128)}), f32[2,1,128,256]{3,0,1,2:T(2,128)S(1)}, u32[]{:S(2)}, u32[]{:S(2)}) async-start(f32[2,1,128,256]{3,0,1,2:T(2,128)} %copy.65), calls=%async_computation.3 | async-start | bytes 524288 | tf_op jit(solution)/shard_map/all_to_all | solution.py:86
  86.9 0.8 copy.68
  87.8 8.2 %all-to-all-done.3 = f32[2,1,128,256]{3,0,1,2:T(2,128)S(1)} async-done(((f32[2,1,128,256]{3,0,1,2:T(2,128)}), f32[2,1,128,256]{3,0,1,2:T(2,128)S(1)}, u32[]{:S(2)}, u32[]{:S(2)}) %all-to-all-start.3) | async-done | bytes 262176 | tf_op jit(solution)/shard_map/all_to_all | solution.py:86
  96.0 3.6 %all-to-all-start.4 = ((f32[2,1,128,256]{3,0,1,2:T(2,128)}), f32[2,1,128,256]{3,0,1,2:T(2,128)S(1)}, u32[]{:S(2)}, u32[]{:S(2)}) async-start(f32[2,1,128,256]{3,0,1,2:T(2,128)} %copy.68), calls=%async_computation.4 | async-start | bytes 524288 | tf_op jit(solution)/shard_map/all_to_all | solution.py:87
  99.6 0.5 fusion.26
  100.2 8.0 %all-to-all-done.4 = f32[2,1,128,256]{3,0,1,2:T(2,128)S(1)} async-done(((f32[2,1,128,256]{3,0,1,2:T(2,128)}), f32[2,1,128,256]{3,0,1,2:T(2,128)S(1)}, u32[]{:S(2)}, u32[]{:S(2)}) %all-to-all-start.4) | async-done | bytes 262176 | tf_op jit(solution)/shard_map/all_to_all | solution.py:87
  108.2 0.5 fusion.22
  108.7 0.5 fusion.5
  109.3 0.5 fusion.4
  109.9 1.0 copy.73
  110.8 3.6 %all-to-all-start.5 = ((f32[4,8,16,256]{3,2,0,1:T(8,128)}), f32[4,8,16,256]{3,2,0,1:T(8,128)S(1)}, u32[]{:S(2)}, u32[]{:S(2)}) async-start(f32[4,8,16,256]{3,2,0,1:T(8,128)} %copy.73), calls=%async_computation.5 | async-start | bytes 1048576 | tf_op jit(solution)/shard_map/all_to_all | solution.py:92
  114.4 0.1 fusion.108
  114.5 14.1 %all-to-all-done.5 = f32[4,8,16,256]{3,2,0,1:T(8,128)S(1)} async-done(((f32[4,8,16,256]{3,2,0,1:T(8,128)}), f32[4,8,16,256]{3,2,0,1:T(8,128)S(1)}, u32[]{:S(2)}, u32[]{:S(2)}) %all-to-all-start.5) | async-done | bytes 524320 | tf_op jit(solution)/shard_map/all_to_all | solution.py:92
  128.6 0.0 copy-start.5
  128.6 0.7 copy-done.5
  129.2 0.8 fusion.30
  (17 shorter events, 0.4 us)
Async XLA Ops:
  0.0 7.4 %copy-start = (f32[128,256]{1,0:T(8,128)S(1)}, f32[128,256]{1,0:T(8,128)}, u32[]{:S(2)}) copy-start(f32[128,256]{1,0:T(8,128)} %param.8) | copy-start | bytes 393220
  0.0 7.4 %copy-start.1 = (f32[128,256]{1,0:T(8,128)S(1)}, f32[128,256]{1,0:T(8,128)}, u32[]{:S(2)}) copy-start(f32[128,256]{1,0:T(8,128)} %param.7) | copy-start | bytes 393220
  0.0 7.4 %copy-start.2 = (f32[128,256]{1,0:T(8,128)S(1)}, f32[128,256]{1,0:T(8,128)}, u32[]{:S(2)}) copy-start(f32[128,256]{1,0:T(8,128)} %param.6) | copy-start | bytes 393220
  1.1 4.9 %copy-start.4 = (f32[3,256]{1,0:T(4,128)S(1)}, f32[3,256]{1,0:T(4,128)}, u32[]{:S(2)}) copy-start(f32[3,256]{1,0:T(4,128)} %param.10) | copy-start | bytes 9220
  1.1 6.2 %collective-permute-start = (f32[3,2,256]{2,1,0:T(2,128)S(1)}, f32[3,2,256]{2,1,0:T(2,128)S(1)}, u32[]{:S(2)}, u32[]{:S(2)}) collective-permute-start(f32[3,2,256]{2,1,0:T(2,128)S(1)} %slice.95), channel_id=1, source_target_pairs={{0,4},{4,8},{8,12},{12,16},{16,20},{20,24},{24,28},{1,5},{5,9},{9,... | collective-permute-start | bytes 18440 | tf_op jit(solution)/shard_map/ppermute | solution.py:12
  7.6 0.9 copy-start.3
  10.2 25.7 %all-to-all-start = ((f32[2,3,1,128,256]{4,0,2,1,3:T(2,128)}), f32[2,3,1,128,256]{4,0,2,1,3:T(2,128)S(1)}, u32[]{:S(2)}, u32[]{:S(2)}) async-start(f32[2,3,1,128,256]{4,0,2,1,3:T(2,128)} %copy.53), calls=%async_computation | async-start | bytes 1572864 | tf_op jit(solution)/shard_map/all_to_all | solution.py:52
  40.3 17.9 %all-to-all-start.1 = ((f32[2,2,8,16,256]{4,3,1,0,2:T(8,128)}), f32[2,2,8,16,256]{4,3,1,0,2:T(8,128)S(1)}, u32[]{:S(2)}, u32[]{:S(2)}) async-start(f32[2,2,8,16,256]{4,3,1,0,2:T(8,128)} %copy.57), calls=%async_computation.1 | async-start | bytes 1048576 | tf_op jit(solution)/shard_map/all_to_all | solution.py:67
  58.2 18.3 %all-to-all-start.2 = ((f32[2,2,8,16,256]{4,3,1,0,2:T(8,128)}), f32[2,2,8,16,256]{4,3,1,0,2:T(8,128)S(1)}, u32[]{:S(2)}, u32[]{:S(2)}) async-start(f32[2,2,8,16,256]{4,3,1,0,2:T(8,128)} %copy.60), calls=%async_computation.2 | async-start | bytes 1048576 | tf_op jit(solution)/shard_map/all_to_all | solution.py:68
  83.3 12.7 %all-to-all-start.3 = ((f32[2,1,128,256]{3,0,1,2:T(2,128)}), f32[2,1,128,256]{3,0,1,2:T(2,128)S(1)}, u32[]{:S(2)}, u32[]{:S(2)}) async-start(f32[2,1,128,256]{3,0,1,2:T(2,128)} %copy.65), calls=%async_computation.3 | async-start | bytes 524288 | tf_op jit(solution)/shard_map/all_to_all | solution.py:86
  96.0 12.2 %all-to-all-start.4 = ((f32[2,1,128,256]{3,0,1,2:T(2,128)}), f32[2,1,128,256]{3,0,1,2:T(2,128)S(1)}, u32[]{:S(2)}, u32[]{:S(2)}) async-start(f32[2,1,128,256]{3,0,1,2:T(2,128)} %copy.68), calls=%async_computation.4 | async-start | bytes 524288 | tf_op jit(solution)/shard_map/all_to_all | solution.py:87
  110.8 17.7 %all-to-all-start.5 = ((f32[4,8,16,256]{3,2,0,1:T(8,128)}), f32[4,8,16,256]{3,2,0,1:T(8,128)S(1)}, u32[]{:S(2)}, u32[]{:S(2)}) async-start(f32[4,8,16,256]{3,2,0,1:T(8,128)} %copy.73), calls=%async_computation.5 | async-start | bytes 1048576 | tf_op jit(solution)/shard_map/all_to_all | solution.py:92
  128.6 0.7 copy-start.5
where the time goes:
time: 131 us; the launch traced here: 130 us
  waiting for transfers between devices  77.2 us (59%)
  starting transfers between devices  29.5 us (23%)
  matrix products  12.3 us (9%)
  local copies, waits for them, and re-layouts  7.97 us (6%)
  other arithmetic  2.65 us (2%)
    all_to_all x1, waiting for transfers between devices, body(): lax.all_to_all(lifted, 'seq', split_axis=3, concat_axis=2, tiled=True)  19 us
    all_to_all x1, waiting for transfers between devices, body(): lax.all_to_all(packed, 'seq', split_axis=1, concat_axis=2, tiled=True)  14.1 us
    all_to_all x1, waiting for transfers between devices, body(): lax.all_to_all(real_part, 'seq', split_axis=2, concat_axis=3, tiled=True)  13.4 us
    all_to_all x1, waiting for transfers between devices, body(): lax.all_to_all(imag_part, 'seq', split_axis=2, concat_axis=3, tiled=True)  13.4 us
    all_to_all x1, waiting for transfers between devices, body(): lax.all_to_all(back_real, 'seq', split_axis=2, concat_axis=1, tiled=True)  8.24 us
    all_to_all x1, waiting for transfers between devices, body(): lax.all_to_all(back_imag, 'seq', split_axis=2, concat_axis=1, tiled=True)  8.02 us
    all_to_all x1, starting transfers between devices, body(): lax.all_to_all(lifted, 'seq', split_axis=3, concat_axis=2, tiled=True)  6.6 us
    ppermute x1, starting transfers between devices, passed_along(): return lax.ppermute(block, axis, route)  4.9 us
  transfers between devices with their start and end apart: 7, of which 7 were waited for; matrix products, arithmetic and copies ran while one was open for 3% of the time, Pallas kernels for 0%

commit v1 on v0

--- a/solution.py
+++ b/solution.py
@@ -1,8 +1,12 @@
+import functools
 import math
 
 import jax
 import jax.numpy as jnp
+import numpy as np
 from jax import lax
+from jax.experimental import pallas as pl
+from jax.experimental.pallas import tpu as pltpu
 from jax.sharding import PartitionSpec as P
 
 
@@ -25,7 +29,7 @@
     return (first - second, third + fourth)
 
 
-def body(queries, keys, values, filters, short_w, bias):
+def spread_body(queries, keys, values, filters, short_w, bias):
     row_count, channels = queries.shape
     shards = lax.axis_size("seq")
     device = lax.axis_index("seq")
@@ -97,6 +101,254 @@
     return shorted[0] * (long_part + bias * gated)
 
 
+MESH = pl.DeviceIdType.MESH
+HALO = 8
+GROUPS = 2
+
+
+def mirrored(index, mask):
+    weight = 1
+    flipped = index
+    while weight <= mask:
+        if mask & weight:
+            flipped = flipped + weight * (1 - 2 * ((index // weight) % 2))
+        weight *= 2
+    return flipped
+
+
+@functools.lru_cache(maxsize=None)
+def tables(blocks, lanes):
+    total = blocks * lanes
+    index = np.arange(lanes)
+    phase = 2.0 * np.pi * ((index[:, None] * index[None, :]) % lanes) / lanes
+    cosine, sine = np.cos(phase), np.sin(phase)
+    matrix = np.block([[cosine, -sine], [sine, cosine]]).astype(np.float32)
+    high = matrix.astype(jnp.bfloat16)
+    low = (matrix - high.astype(np.float32)).astype(jnp.bfloat16)
+    turn = -2.0 * np.pi * (np.arange(blocks) + 0.25)[:, None] * index[None, :] / total
+    twist = np.stack((np.cos(turn), np.sin(turn))).astype(np.float32)
+    return np.stack((high, low)), np.repeat(twist[:, :, None, :], 8, axis=2)
+
+
+def roots(blocks):
+    turn = -2.0 * np.pi * (np.arange(blocks) + 0.25)[:, None] * np.arange(blocks)[None, :] / blocks
+    return np.cos(turn), np.sin(turn)
+
+
+def weighted(terms):
+    total = None
+    for scale, term in terms:
+        part = term * np.float32(scale)
+        total = part if total is None else total + part
+    return total
+
+
+def split_dot(rows, matrix):
+    high = rows.astype(jnp.bfloat16)
+    low = (rows - high.astype(jnp.float32)).astype(jnp.bfloat16)
+
+    def dot(left, right):
+        return jnp.dot(left, right, preferred_element_type=jnp.float32)
+
+    return dot(high, matrix[0]) + (dot(low, matrix[0]) + dot(high, matrix[1]))
+
+
+def kernel(
+    blocks,
+    q_hbm, k_hbm, v_hbm, f_hbm, w_hbm, bias_hbm, matrix_hbm, twist_hbm,
+    out_ref,
+    q_ref, k_ref, v_ref, f_ref, w_ref, bias_ref, matrix_ref, twist_ref,
+    halo, ext, gated, f_sent, g_sent, f_all, g_all, spectrum, y_sent, y_all, q_short,
+    load_sem, halo_send, halo_recv, f_send, f_recv, g_send, g_recv, y_send, y_recv,
+):
+    me = lax.axis_index("seq")
+    rows, channels = out_ref.shape
+    owned = channels // blocks
+    part = owned // GROUPS
+    pairs = (
+        (f_hbm, f_ref), (k_hbm, k_ref), (v_hbm, v_ref), (w_hbm, w_ref),
+        (q_hbm, q_ref), (matrix_hbm, matrix_ref), (twist_hbm, twist_ref), (bias_hbm, bias_ref),
+    )
+    loads = [pltpu.make_async_copy(src, dst, load_sem.at[i]) for i, (src, dst) in enumerate(pairs)]
+    for load in loads:
+        load.start()
+    barrier = pltpu.get_barrier_semaphore()
+    masks = list(range(blocks - 1, 0, -1))
+    for mask in masks:
+        pl.semaphore_signal(barrier, inc=1, device_id={"seq": mirrored(me, mask)}, device_id_type=MESH)
+
+    def to_owner(sent, landed, send, recv, mask, group):
+        peer = mirrored(me, mask)
+        span = pl.ds(group * part, part)
+        return pltpu.make_async_remote_copy(
+            src_ref=sent.at[peer, span],
+            dst_ref=landed.at[me, span],
+            send_sem=send.at[group, mask],
+            recv_sem=recv.at[group, mask],
+            device_id={"seq": peer},
+            device_id_type=MESH,
+        )
+
+    def halo_copy(which, stream):
+        return pltpu.make_async_remote_copy(
+            src_ref=stream.at[pl.ds(rows - HALO, HALO)],
+            dst_ref=halo.at[which],
+            send_sem=halo_send.at[which],
+            recv_sem=halo_recv.at[which],
+            device_id={"seq": lax.rem(me + 1, blocks)},
+            device_id_type=MESH,
+        )
+
+    streams = (k_ref, v_ref, q_ref)
+    loads[0].wait()
+    f_sent[...] = jnp.transpose(f_ref[...]).reshape(blocks, owned, rows)
+    loads[1].wait()
+    loads[2].wait()
+    loads[3].wait()
+    loads[4].wait()
+    pl.semaphore_wait(barrier, blocks - 1)
+
+    @pl.when(me < blocks - 1)
+    def _():
+        for which, stream in enumerate(streams):
+            halo_copy(which, stream).start()
+
+    f_copies = [to_owner(f_sent, f_all, f_send, f_recv, mask, group) for group in range(GROUPS) for mask in masks]
+    for copy in f_copies:
+        copy.start()
+    f_all[me] = f_sent[me]
+
+    def shorted(stream, which):
+        ext[which, pl.ds(0, HALO)] = jnp.where(me == 0, jnp.zeros((HALO, channels), jnp.float32), halo[which])
+        ext[which, pl.ds(HALO, rows)] = stream[...]
+        taps = w_ref[...]
+        return (
+            taps[0:1] * ext[which, pl.ds(HALO, rows)]
+            + taps[1:2] * ext[which, pl.ds(HALO - 1, rows)]
+            + taps[2:3] * ext[which, pl.ds(HALO - 2, rows)]
+        )
+
+    @pl.when(me == 0)
+    def _():
+        halo[...] = jnp.zeros_like(halo)
+
+    @pl.when(me > 0)
+    def _():
+        for which, stream in enumerate(streams):
+            halo_copy(which, stream).wait_recv()
+
+    gated[...] = shorted(k_ref, 0) * shorted(v_ref, 1)
+    g_sent[...] = jnp.transpose(gated[...]).reshape(blocks, owned, rows)
+    g_copies = [[to_owner(g_sent, g_all, g_send, g_recv, mask, group) for mask in masks] for group in range(GROUPS)]
+    for group in range(GROUPS):
+        for copy in g_copies[group]:
+            copy.start()
+    g_all[me] = g_sent[me]
+    q_short[...] = shorted(q_ref, 2)
+    for load in loads[5:]:
+        load.wait()
+
+    root_re, root_im = roots(blocks)
+
+    def twisted(real, imag, step):
+        twist_re = jnp.concatenate([twist_ref[0, step]] * (part // 8), axis=0)
+        twist_im = jnp.concatenate([twist_ref[1, step]] * (part // 8), axis=0)
+        return real * twist_re - imag * twist_im, real * twist_im + imag * twist_re
+
+    def transformed(signal, group):
+        span = pl.ds(group * part, part)
+        held = [signal[a, span] for a in range(blocks)]
+        mixed = []
+        for step in range(blocks):
+            real = weighted([(root_re[step, a], held[a]) for a in range(blocks)])
+            imag = weighted([(root_im[step, a], held[a]) for a in range(blocks)])
+            mixed.append(jnp.concatenate(twisted(real, imag, step), axis=1))
+        return split_dot(jnp.concatenate(mixed, axis=0), matrix_ref)
+
+    for group in range(GROUPS):
+        for index, mask in enumerate(masks):
+            f_copies[group * len(masks) + index].wait_recv()
+        spectrum[group] = transformed(f_all, group)
+    scale = 1.0 / (blocks * rows)
+    y_copies = []
+    for group in range(GROUPS):
+        span = pl.ds(group * part, part)
+        for copy in g_copies[group]:
+            copy.wait_recv()
+        other = transformed(g_all, group)
+        f_re, f_im = spectrum[group, :, :rows], spectrum[group, :, rows:]
+        g_re, g_im = other[:, :rows], other[:, rows:]
+        product = jnp.concatenate((f_re * g_re - f_im * g_im, -(f_re * g_im + f_im * g_re)), axis=1)
+        back = split_dot(product, matrix_ref)
+        turned = []
+        for step in range(blocks):
+            piece = back[step * part : (step + 1) * part]
+            turned.append(twisted(piece[:, :rows], piece[:, rows:], step))
+        for a in range(blocks):
+            terms = [(scale * root_re[step, a], turned[step][0]) for step in range(blocks)]
+            terms += [(-scale * root_im[step, a], turned[step][1]) for step in range(blocks)]
+            y_sent[a, span] = weighted(terms)
+        for mask in masks:
+            copy = to_owner(y_sent, y_all, y_send, y_recv, mask, group)
+            copy.start()
+            y_copies.append(copy)
+        y_all[me, span] = y_sent[me, span]
+    for copy in y_copies:
+        copy.wait_recv()
+    long = jnp.transpose(y_all[...].reshape(channels, rows))
+    out_ref[...] = q_short[...] * (long + bias_ref[...][None, :] * gated[...])
+    for copy in f_copies + g_copies[0] + [c for later in g_copies[1:] for c in later] + y_copies:
+        copy.wait_send()
+
+    @pl.when(me < blocks - 1)
+    def _():
+        for which, stream in enumerate(streams):
+            halo_copy(which, stream).wait_send()
+
+
+def owner_body(queries, keys, values, filters, short_w, bias):
+    rows, channels = queries.shape
+    blocks = lax.axis_size("seq")
+    owned = channels // blocks
+    matrix, twist = tables(blocks, rows)
+    float32 = jnp.float32
+    block_buffer = pltpu.VMEM((blocks, owned, rows), float32)
+    stream_buffer = pltpu.VMEM((rows, channels), float32)
+    by_copy = pltpu.SemaphoreType.DMA((GROUPS, blocks))
+    return pl.pallas_call(
+        functools.partial(kernel, blocks),
+        out_shape=jax.ShapeDtypeStruct((rows, channels), float32),
+        in_specs=[pl.BlockSpec(memory_space=pl.ANY)] * 8,
+        out_specs=pl.BlockSpec(memory_space=pltpu.VMEM),
+        scratch_shapes=[stream_buffer] * 4
+        + [
+            pltpu.VMEM(short_w.shape, float32),
+            pltpu.VMEM(bias.shape, float32),
+            pltpu.VMEM(matrix.shape, jnp.bfloat16),
+            pltpu.VMEM(twist.shape, float32),
+            pltpu.VMEM((3, HALO, channels), float32),
+            pltpu.VMEM((3, HALO + rows, channels), float32),
+            stream_buffer,
+        ]
+        + [block_buffer] * 4
+        + [pltpu.VMEM((GROUPS, channels // GROUPS, 2 * rows), float32)]
+        + [block_buffer] * 2
+        + [stream_buffer, pltpu.SemaphoreType.DMA((8,))]
+        + [pltpu.SemaphoreType.DMA((3,))] * 2
+        + [by_copy] * 6,
+        compiler_params=pltpu.CompilerParams(collective_id=0, has_side_effects=True),
+    )(queries, keys, values, filters, short_w, bias, jnp.asarray(matrix), jnp.asarray(twist))
+
+
+def body(queries, keys, values, filters, short_w, bias):
+    rows, channels = queries.shape
+    blocks = lax.axis_size("seq")
+    whole_tiles = channels % (blocks * GROUPS * 8) == 0 and rows % 128 == 0
+    if whole_tiles and blocks & (blocks - 1) == 0:
+        return owner_body(queries, keys, values, filters, short_w, bias)
+    return spread_body(queries, keys, values, filters, short_w, bias)
+
+
 def solution(mesh):
     placed = (
         P("seq", "ch"),

time: 131 us -> 21.8 us (0.17)
  waiting for transfers between devices: 77.2 us -> 0 us
  starting transfers between devices: 29.5 us -> 0 us
  Pallas kernels: 0 us -> 20.1 us
  matrix products: 12.3 us -> 0 us
  local copies, waits for them, and re-layouts: 7.97 us -> 1.57 us
  other arithmetic: 2.65 us -> 0 us
    all_to_all x6 -> x0, waiting for transfers between devices: 76 us -> none  [the longest x1 19 us: body(): lax.all_to_all(lifted, 'seq', split_axis=3, concat_axis=2, tiled=True)]
    all_to_all x6 -> x0, starting transfers between devices: 24.6 us -> none  [the longest x1 6.6 us: body(): lax.all_to_all(lifted, 'seq', split_axis=3, concat_axis=2, tiled=True)]
    pallas_call x0 -> x1, Pallas kernels: none -> 20.1 us  [owner_body(): pl.pallas_call(functools.partial(kernel, blocks), out_shape=jax.ShapeDtyp...]
    dot_general x16 -> x0, matrix products: 12.3 us -> none  [the longest x4 3.13 us: complex_mix(): jnp.einsum(form, mat_imag, data_real, precision=lax.Precision.HIGHEST)]
    ppermute x1 -> x0, starting transfers between devices: 4.9 us -> none  [passed_along(): return lax.ppermute(block, axis, route)]
    add x2 -> x0, local copies, waits for them, and re-layouts: 1.82 us -> none  [the longest x1 0.97 us: body(): real_part * twist_sin + imag_part * twist_cos]
    sub x2 -> x0, local copies, waits for them, and re-layouts: 1.8 us -> none  [the longest x1 0.98 us: body(): real_part * twist_cos - imag_part * twist_sin]
    broadcast_in_dim x1 -> x0, local copies, waits for them, and re-layouts: 1.5 us -> none  [body(): jnp.stack((signal, signal * cosine[:, None], signal * sine[:, None]), axi...]
  transfers between devices with their start and end apart: 7 -> 0, of which waited for: 7 -> 0; matrix products, arithmetic and copies ran while one was open for 3% -> 0% of each run, Pallas kernels for 0% -> 0%
where the time goes in v1:
time: 21.8 us; the launch traced here: 21.7 us
  Pallas kernels  20.1 us (92%)
  local copies, waits for them, and re-layouts  1.57 us (7%)
    pallas_call x1, Pallas kernels, owner_body(): pl.pallas_call(functools.partial(kernel, blocks), out_shape=jax.ShapeDtyp...  20.1 us
    unnamed x1, local copies, waits for them, and re-layouts  1.57 us

profile of v1, /device:TPU:0, one launch (start us, length us, event | category | flops | bytes accessed | tf_op | source)
XLA Modules:
  0.0 21.7 jit_solution(8012207628316855628)
XLA Ops:
  0.0 20.1 %shard_map.82 = f32[128,256]{1,0:T(8,128)} custom-call(f32[128,256]{1,0:T(8,128)} %q_hbm.1, f32[128,256]{1,0:T(8,128)} %k_hbm.1, f32[128,256]{1,0:T(8,128)} %v_hbm.1, f32[128,256]{1,0:T(8,128)} %f_hbm.1, f32[3,256]{1,0:T(4,128)} %w_hbm.1, f32[256]{0:T(256)} %bias_hbm.1, bf16[2,256,256]{2,1,0:T(8,128)(2,1)} %constant.4.clone.matrix_hbm, ...), custom_call_target="tpu_custom_call" | custom-call | tf_op jit(solution)/shard_map/pallas_call | solution.py:318
  20.1 1.6 %copy.10 = f32[128,256]{1,0:T(8,128)} copy(f32[128,256]{1,0:T(8,128)} %shard_map.82) | data formatting | bytes 262144

commit v2 on v1

--- a/solution.py
+++ b/solution.py
@@ -103,7 +103,9 @@
 
 MESH = pl.DeviceIdType.MESH
 HALO = 8
-GROUPS = 2
+VMEM_LIMIT = 4 * 1024 * 1024
+F_GROUPS, G_GROUPS, Y_GROUPS = 1, 2, 2
+GROUPS = max(F_GROUPS, G_GROUPS, Y_GROUPS)
 
 
 def mirrored(index, mask):
@@ -165,6 +167,10 @@
     rows, channels = out_ref.shape
     owned = channels // blocks
     part = owned // GROUPS
+    masks = list(range(blocks - 1, 0, -1))
+    barrier = pltpu.get_barrier_semaphore()
+    for mask in masks:
+        pl.semaphore_signal(barrier, inc=1, device_id={"seq": mirrored(me, mask)}, device_id_type=MESH)
     pairs = (
         (f_hbm, f_ref), (k_hbm, k_ref), (v_hbm, v_ref), (w_hbm, w_ref),
         (q_hbm, q_ref), (matrix_hbm, matrix_ref), (twist_hbm, twist_ref), (bias_hbm, bias_ref),
@@ -172,14 +178,11 @@
     loads = [pltpu.make_async_copy(src, dst, load_sem.at[i]) for i, (src, dst) in enumerate(pairs)]
     for load in loads:
         load.start()
-    barrier = pltpu.get_barrier_semaphore()
-    masks = list(range(blocks - 1, 0, -1))
-    for mask in masks:
-        pl.semaphore_signal(barrier, inc=1, device_id={"seq": mirrored(me, mask)}, device_id_type=MESH)
-
-    def to_owner(sent, landed, send, recv, mask, group):
+
+    def to_owner(sent, landed, send, recv, mask, group, groups):
         peer = mirrored(me, mask)
-        span = pl.ds(group * part, part)
+        share = owned // groups
+        span = pl.ds(group * share, share)
         return pltpu.make_async_remote_copy(
             src_ref=sent.at[peer, span],
             dst_ref=landed.at[me, span],
@@ -202,51 +205,61 @@
     streams = (k_ref, v_ref, q_ref)
     loads[0].wait()
     f_sent[...] = jnp.transpose(f_ref[...]).reshape(blocks, owned, rows)
-    loads[1].wait()
-    loads[2].wait()
-    loads[3].wait()
-    loads[4].wait()
+    f_all[me] = f_sent[me]
+    for load in loads[1:4]:
+        load.wait()
+    taps = w_ref[...]
+
+    def shorted(which, count):
+        return (
+            taps[0:1] * ext[which, pl.ds(HALO, count)]
+            + taps[1:2] * ext[which, pl.ds(HALO - 1, count)]
+            + taps[2:3] * ext[which, pl.ds(HALO - 2, count)]
+        )
+
+    @pl.when(me == 0)
+    def _():
+        halo[...] = jnp.zeros_like(halo)
+
+    for which, stream in enumerate(streams[:2]):
+        ext[which, pl.ds(0, HALO)] = jnp.zeros((HALO, channels), jnp.float32)
+        ext[which, pl.ds(HALO, rows)] = stream[...]
+    gated[...] = shorted(0, rows) * shorted(1, rows)
+    g_sent[...] = jnp.transpose(gated[...]).reshape(blocks, owned, rows)
     pl.semaphore_wait(barrier, blocks - 1)
 
     @pl.when(me < blocks - 1)
     def _():
-        for which, stream in enumerate(streams):
-            halo_copy(which, stream).start()
-
-    f_copies = [to_owner(f_sent, f_all, f_send, f_recv, mask, group) for group in range(GROUPS) for mask in masks]
+        halo_copy(0, k_ref).start()
+        halo_copy(1, v_ref).start()
+
+    f_copies = [to_owner(f_sent, f_all, f_send, f_recv, mask, 0, 1) for mask in masks]
     for copy in f_copies:
         copy.start()
-    f_all[me] = f_sent[me]
-
-    def shorted(stream, which):
-        ext[which, pl.ds(0, HALO)] = jnp.where(me == 0, jnp.zeros((HALO, channels), jnp.float32), halo[which])
-        ext[which, pl.ds(HALO, rows)] = stream[...]
-        taps = w_ref[...]
-        return (
-            taps[0:1] * ext[which, pl.ds(HALO, rows)]
-            + taps[1:2] * ext[which, pl.ds(HALO - 1, rows)]
-            + taps[2:3] * ext[which, pl.ds(HALO - 2, rows)]
-        )
-
-    @pl.when(me == 0)
-    def _():
-        halo[...] = jnp.zeros_like(halo)
 
     @pl.when(me > 0)
     def _():
-        for which, stream in enumerate(streams):
-            halo_copy(which, stream).wait_recv()
-
-    gated[...] = shorted(k_ref, 0) * shorted(v_ref, 1)
-    g_sent[...] = jnp.transpose(gated[...]).reshape(blocks, owned, rows)
-    g_copies = [[to_owner(g_sent, g_all, g_send, g_recv, mask, group) for mask in masks] for group in range(GROUPS)]
-    for group in range(GROUPS):
+        halo_copy(0, k_ref).wait_recv()
+        halo_copy(1, v_ref).wait_recv()
+
+    for which in range(2):
+        ext[which, pl.ds(0, HALO)] = halo[which]
+    first = shorted(0, HALO) * shorted(1, HALO)
+    gated[pl.ds(0, HALO)] = first
+    g_sent[:, :, pl.ds(0, HALO)] = jnp.transpose(first).reshape(blocks, owned, HALO)
+    g_copies = [
+        [to_owner(g_sent, g_all, g_send, g_recv, mask, group, G_GROUPS) for mask in masks] for group in range(G_GROUPS)
+    ]
+    for group in range(G_GROUPS):
         for copy in g_copies[group]:
             copy.start()
     g_all[me] = g_sent[me]
-    q_short[...] = shorted(q_ref, 2)
-    for load in loads[5:]:
+    for load in loads[4:]:
         load.wait()
+
+    @pl.when(me < blocks - 1)
+    def _():
+        halo_copy(2, q_ref).start()
 
     root_re, root_im = roots(blocks)
 
@@ -265,16 +278,17 @@
             mixed.append(jnp.concatenate(twisted(real, imag, step), axis=1))
         return split_dot(jnp.concatenate(mixed, axis=0), matrix_ref)
 
+    for copy in f_copies:
+        copy.wait_recv()
     for group in range(GROUPS):
-        for index, mask in enumerate(masks):
-            f_copies[group * len(masks) + index].wait_recv()
         spectrum[group] = transformed(f_all, group)
     scale = 1.0 / (blocks * rows)
     y_copies = []
     for group in range(GROUPS):
         span = pl.ds(group * part, part)
-        for copy in g_copies[group]:
-            copy.wait_recv()
+        if group % (GROUPS // G_GROUPS) == 0:
+            for copy in g_copies[group // (GROUPS // G_GROUPS)]:
+                copy.wait_recv()
         other = transformed(g_all, group)
         f_re, f_im = spectrum[group, :, :rows], spectrum[group, :, rows:]
         g_re, g_im = other[:, :rows], other[:, rows:]
@@ -288,11 +302,20 @@
             terms = [(scale * root_re[step, a], turned[step][0]) for step in range(blocks)]
             terms += [(-scale * root_im[step, a], turned[step][1]) for step in range(blocks)]
             y_sent[a, span] = weighted(terms)
-        for mask in masks:
-            copy = to_owner(y_sent, y_all, y_send, y_recv, mask, group)
-            copy.start()
-            y_copies.append(copy)
+        if (group + 1) % (GROUPS // Y_GROUPS) == 0:
+            for mask in masks:
+                copy = to_owner(y_sent, y_all, y_send, y_recv, mask, group // (GROUPS // Y_GROUPS), Y_GROUPS)
+                copy.start()
+                y_copies.append(copy)
         y_all[me, span] = y_sent[me, span]
+
+    @pl.when(me > 0)
+    def _():
+        halo_copy(2, q_ref).wait_recv()
+
+    ext[2, pl.ds(0, HALO)] = halo[2]
+    ext[2, pl.ds(HALO, rows)] = q_ref[...]
+    q_short[...] = shorted(2, rows)
     for copy in y_copies:
         copy.wait_recv()
     long = jnp.transpose(y_all[...].reshape(channels, rows))
@@ -315,6 +338,7 @@
     block_buffer = pltpu.VMEM((blocks, owned, rows), float32)
     stream_buffer = pltpu.VMEM((rows, channels), float32)
     by_copy = pltpu.SemaphoreType.DMA((GROUPS, blocks))
+    operands = (queries, keys, values, filters, short_w, bias, jnp.asarray(matrix), jnp.asarray(twist))
     return pl.pallas_call(
         functools.partial(kernel, blocks),
         out_shape=jax.ShapeDtypeStruct((rows, channels), float32),
@@ -336,8 +360,8 @@
         + [stream_buffer, pltpu.SemaphoreType.DMA((8,))]
         + [pltpu.SemaphoreType.DMA((3,))] * 2
         + [by_copy] * 6,
-        compiler_params=pltpu.CompilerParams(collective_id=0, has_side_effects=True),
-    )(queries, keys, values, filters, short_w, bias, jnp.asarray(matrix), jnp.asarray(twist))
+        compiler_params=pltpu.CompilerParams(collective_id=0, has_side_effects=True, vmem_limit_bytes=VMEM_LIMIT),
+    )(*[pltpu.with_memory_space_constraint(operand, pltpu.HBM) for operand in operands])
 
 
 def body(queries, keys, values, filters, short_w, bias):

time: 21.8 us -> 20.3 us (0.931)
  local copies, waits for them, and re-layouts: 1.57 us -> 0.66 us
  Pallas kernels: 20.1 us -> 19.4 us
    unnamed x1, local copies, waits for them, and re-layouts: 1.57 us -> 0.66 us
    pallas_call x1, Pallas kernels: 20.1 us -> 19.4 us  [owner_body(): pl.pallas_call(functools.partial(kernel, blocks), out_shape=jax.ShapeDtyp...]
where the time goes in v2:
time: 20.3 us; the launch traced here: 20.1 us
  Pallas kernels  19.4 us (96%)
  local copies, waits for them, and re-layouts  0.66 us (3%)
    pallas_call x1, Pallas kernels, owner_body(): pl.pallas_call(functools.partial(kernel, blocks), out_shape=jax.ShapeDtyp...  19.4 us
    unnamed x1, local copies, waits for them, and re-layouts  0.66 us

profile of v2, /device:TPU:0, one launch (start us, length us, event | category | flops | bytes accessed | tf_op | source)
XLA Modules:
  0.0 20.1 jit_solution(2431903194735221128)
XLA Ops:
  0.0 19.4 %shard_map.82 = f32[128,256]{1,0:T(8,128)S(1)} custom-call(f32[128,256]{1,0:T(8,128)} %q_hbm.1, f32[128,256]{1,0:T(8,128)} %k_hbm.1, f32[128,256]{1,0:T(8,128)} %v_hbm.1, f32[128,256]{1,0:T(8,128)} %f_hbm.1, f32[3,256]{1,0:T(4,128)} %w_hbm.1, f32[256]{0:T(256)} %bias_hbm.1, bf16[2,256,256]{2,1,0:T(8,128)(2,1)} %constant.4.clone.matrix_hbm, ...), custom_call_target="tpu_custom_call" | custom-call | tf_op jit(solution)/shard_map/pallas_call | solution.py:342
  19.5 0.7 %copy.10 = f32[128,256]{1,0:T(8,128)} copy(f32[128,256]{1,0:T(8,128)S(1)} %shard_map.82) | data formatting | bytes 262144

commit v3 on v2

--- a/solution.py
+++ b/solution.py
@@ -132,17 +132,40 @@
     return np.stack((high, low)), np.repeat(twist[:, :, None, :], 8, axis=2)
 
 
-def roots(blocks):
-    turn = -2.0 * np.pi * (np.arange(blocks) + 0.25)[:, None] * np.arange(blocks)[None, :] / blocks
-    return np.cos(turn), np.sin(turn)
-
-
-def weighted(terms):
-    total = None
-    for scale, term in terms:
-        part = term * np.float32(scale)
-        total = part if total is None else total + part
-    return total
+def root_product(value, turn):
+    real, imag = value
+    cosine, sine = math.cos(2.0 * math.pi * turn), -math.sin(2.0 * math.pi * turn)
+    if turn == 0:
+        return value
+    if imag is None:
+        return real * np.float32(cosine), real * np.float32(sine)
+    if turn == 0.25:
+        return imag, -real
+    if turn == 0.125:
+        return (real + imag) * np.float32(cosine), (imag - real) * np.float32(cosine)
+    if turn == 0.375:
+        return (imag - real) * np.float32(-cosine), (real + imag) * np.float32(cosine)
+    return real * np.float32(cosine) - imag * np.float32(sine), real * np.float32(sine) + imag * np.float32(cosine)
+
+
+def sum_and_difference(left, right):
+    (left_re, left_im), (right_re, right_im) = left, right
+    if left_im is None and right_im is None:
+        return (left_re + right_re, None), (left_re - right_re, None)
+    if left_im is None:
+        return (left_re + right_re, right_im), (left_re - right_re, -right_im)
+    if right_im is None:
+        return (left_re + right_re, left_im), (left_re - right_re, left_im)
+    return (left_re + right_re, left_im + right_im), (left_re - right_re, left_im - right_im)
+
+
+def small_transform(values):
+    count = len(values)
+    if count == 1:
+        return values
+    even, odd = small_transform(values[0::2]), small_transform(values[1::2])
+    pairs = [sum_and_difference(even[k], root_product(odd[k], k / count)) for k in range(count // 2)]
+    return [pair[0] for pair in pairs] + [pair[1] for pair in pairs]
 
 
 def split_dot(rows, matrix):
@@ -206,7 +229,7 @@
     loads[0].wait()
     f_sent[...] = jnp.transpose(f_ref[...]).reshape(blocks, owned, rows)
     f_all[me] = f_sent[me]
-    for load in loads[1:4]:
+    for load in loads[1:5]:
         load.wait()
     taps = w_ref[...]
 
@@ -230,8 +253,8 @@
 
     @pl.when(me < blocks - 1)
     def _():
-        halo_copy(0, k_ref).start()
-        halo_copy(1, v_ref).start()
+        for which, stream in enumerate(streams):
+            halo_copy(which, stream).start()
 
     f_copies = [to_owner(f_sent, f_all, f_send, f_recv, mask, 0, 1) for mask in masks]
     for copy in f_copies:
@@ -254,14 +277,16 @@
         for copy in g_copies[group]:
             copy.start()
     g_all[me] = g_sent[me]
-    for load in loads[4:]:
+    for load in loads[5:]:
         load.wait()
 
-    @pl.when(me < blocks - 1)
+    @pl.when(me > 0)
     def _():
-        halo_copy(2, q_ref).start()
-
-    root_re, root_im = roots(blocks)
+        halo_copy(2, q_ref).wait_recv()
+
+    ext[2, pl.ds(0, HALO)] = halo[2]
+    ext[2, pl.ds(HALO, rows)] = q_ref[...]
+    q_short[...] = shorted(2, rows)
 
     def twisted(real, imag, step):
         twist_re = jnp.concatenate([twist_ref[0, step]] * (part // 8), axis=0)
@@ -271,10 +296,9 @@
     def transformed(signal, group):
         span = pl.ds(group * part, part)
         held = [signal[a, span] for a in range(blocks)]
+        turned = [root_product((held[a], None), a / (4 * blocks)) for a in range(blocks)]
         mixed = []
-        for step in range(blocks):
-            real = weighted([(root_re[step, a], held[a]) for a in range(blocks)])
-            imag = weighted([(root_im[step, a], held[a]) for a in range(blocks)])
+        for step, (real, imag) in enumerate(small_transform(turned)):
             mixed.append(jnp.concatenate(twisted(real, imag, step), axis=1))
         return split_dot(jnp.concatenate(mixed, axis=0), matrix_ref)
 
@@ -298,28 +322,20 @@
         for step in range(blocks):
             piece = back[step * part : (step + 1) * part]
             turned.append(twisted(piece[:, :rows], piece[:, rows:], step))
-        for a in range(blocks):
-            terms = [(scale * root_re[step, a], turned[step][0]) for step in range(blocks)]
-            terms += [(-scale * root_im[step, a], turned[step][1]) for step in range(blocks)]
-            y_sent[a, span] = weighted(terms)
+        for a, (real, imag) in enumerate(small_transform(turned)):
+            turn = 2.0 * math.pi * a / (4 * blocks)
+            y_sent[a, span] = real * np.float32(scale * math.cos(turn)) + imag * np.float32(scale * math.sin(turn))
         if (group + 1) % (GROUPS // Y_GROUPS) == 0:
             for mask in masks:
                 copy = to_owner(y_sent, y_all, y_send, y_recv, mask, group // (GROUPS // Y_GROUPS), Y_GROUPS)
                 copy.start()
                 y_copies.append(copy)
         y_all[me, span] = y_sent[me, span]
-
-    @pl.when(me > 0)
-    def _():
-        halo_copy(2, q_ref).wait_recv()
-
-    ext[2, pl.ds(0, HALO)] = halo[2]
-    ext[2, pl.ds(HALO, rows)] = q_ref[...]
-    q_short[...] = shorted(2, rows)
+    gated[...] = gated[...] * bias_ref[...][None, :]
     for copy in y_copies:
         copy.wait_recv()
     long = jnp.transpose(y_all[...].reshape(channels, rows))
-    out_ref[...] = q_short[...] * (long + bias_ref[...][None, :] * gated[...])
+    out_ref[...] = q_short[...] * (long + gated[...])
     for copy in f_copies + g_copies[0] + [c for later in g_copies[1:] for c in later] + y_copies:
         copy.wait_send()
 

time: 20.3 us -> 20.2 us (level)
  no operation moved by 1% of the time
where the time goes in v3:
time: 20.2 us; the launch traced here: 20.1 us
  Pallas kernels  19.4 us (96%)
  local copies, waits for them, and re-layouts  0.66 us (3%)
    pallas_call x1, Pallas kernels, owner_body(): pl.pallas_call(functools.partial(kernel, blocks), out_shape=jax.ShapeDtyp...  19.4 us
    unnamed x1, local copies, waits for them, and re-layouts  0.66 us

profile of v3, /device:TPU:0, one launch (start us, length us, event | category | flops | bytes accessed | tf_op | source)
XLA Modules:
  0.0 20.1 jit_solution(3813713503343171269)
XLA Ops:
  0.0 19.4 %shard_map.82 = f32[128,256]{1,0:T(8,128)S(1)} custom-call(f32[128,256]{1,0:T(8,128)} %q_hbm.1, f32[128,256]{1,0:T(8,128)} %k_hbm.1, f32[128,256]{1,0:T(8,128)} %v_hbm.1, f32[128,256]{1,0:T(8,128)} %f_hbm.1, f32[3,256]{1,0:T(4,128)} %w_hbm.1, f32[256]{0:T(256)} %bias_hbm.1, bf16[2,256,256]{2,1,0:T(8,128)(2,1)} %constant.4.clone.matrix_hbm, ...), custom_call_target="tpu_custom_call" | custom-call | tf_op jit(solution)/shard_map/pallas_call | solution.py:358
  19.4 0.7 %copy.10 = f32[128,256]{1,0:T(8,128)} copy(f32[128,256]{1,0:T(8,128)S(1)} %shard_map.82) | data formatting | bytes 262144
